TPU v7x, 256 devices: a whole 4x4x8 slice. The times are simulated.
256 devices in a mesh: row: 16 (over x_hi, y, core), col: 16 (over z, x_lo).
Axes of the slice: x: 4 (x_hi: 2, x_lo: 2; x = x_hi * 2 + x_lo), y: 4, z: 8, core: 2. Of those that a mesh axis runs over, the one named last changes fastest.
Arguments:
- vectors: float32 [16, 32768], P(None, ('col', 'row')), may hold values from -6 to 6
- tile_blocks: float32 [16, 16, 128, 128, 128], P('row', 'col'), may hold values from -0.046875 to 0.046875
- coords: int32 [16, 16, 128], P('row', 'col'), may hold values from 0 to 255, as said below
- counts: int32 [16, 16], P('row', 'col'), may hold values from 1 to 128, as said below
Outputs:
- product: float32 [16, 32768], P(None, ('col', 'row'))
Inputs may be any that keep to these rules, and one draw needn't show every extreme that they name: `counts`: every cell has at least one live slot and some cell has exactly 128. `coords`: within one cell all 128 entries are distinct; slots at or past counts hold no tile of S.
All inputs are finite; a program needn't handle non-finite values.
Results may differ from a plain program's by a relative error of at most 0.0003.
Values sent between devices are 32-bit elements; how exact they have to be, the bound alone decides.
No kernel may reach another device: no remote copies, remote signals or barrier semaphores. Data moves between devices by JAX's collectives and lax.ppermute only.
A program may use at most 64 MiB of HBM per device.

v0:
```python
import jax
import jax.numpy as jnp
from jax import lax
from jax.sharding import PartitionSpec as P

HIGH = lax.Precision.HIGHEST


def from_root(value, axis, source):
    kept = jnp.where(lax.axis_index(axis) == source, value, 0).astype(value.dtype)
    return lax.psum(kept, axis)


def slot_terms(blocks, slot_coords, live_mask, x_col, x_row):
    vec_count = x_col.shape[0]
    tile_size = blocks.shape[-1]
    seg_tiles = x_row.shape[1] // tile_size
    col_tiles = x_col.shape[1] // tile_size
    row_pos = slot_coords // col_tiles
    col_pos = slot_coords % col_tiles
    picked_col = jnp.take(x_col.reshape(vec_count, col_tiles, tile_size), col_pos, axis=1)
    picked_row = jnp.take(x_row.reshape(vec_count, seg_tiles, tile_size), row_pos, axis=1)
    normal = jnp.einsum("vsk,smk->vsm", picked_col, blocks, precision=HIGH)
    transposed = jnp.einsum("vsm,smk->vsk", picked_row, blocks, precision=HIGH)
    onehot_rows = (row_pos[:, None] == jnp.arange(seg_tiles, dtype=jnp.int32)[None, :]).astype(
        jnp.float32
    ) * live_mask[:, None]
    onehot_cols = (col_pos[:, None] == jnp.arange(col_tiles, dtype=jnp.int32)[None, :]).astype(
        jnp.float32
    ) * live_mask[:, None]
    row_terms = jnp.einsum("st,vsm->vtm", onehot_rows, normal, precision=HIGH).reshape(
        vec_count, seg_tiles * tile_size
    )
    col_terms = jnp.einsum("st,vsk->vtk", onehot_cols, transposed, precision=HIGH).reshape(
        vec_count, col_tiles * tile_size
    )
    return (row_terms, col_terms)


def local(vectors, tile_blocks, coords, counts):
    n_row = lax.axis_size("row")
    n_col = lax.axis_size("col")
    seg_ratio = n_row // n_col
    max_slots = tile_blocks.shape[2]
    tile_size = tile_blocks.shape[-1]
    blocks = tile_blocks.reshape(max_slots, tile_size, tile_size)
    slot_coords = coords.reshape(max_slots)
    slot_count = counts.reshape(())
    row_idx = lax.axis_index("row")
    col_idx = lax.axis_index("col")
    x_col = lax.all_gather(vectors, "row", axis=1, tiled=True)
    x_row = from_root(x_col, "col", row_idx // seg_ratio)
    live_mask = (jnp.arange(max_slots, dtype=jnp.int32) < slot_count).astype(jnp.float32)
    row_terms, col_terms = slot_terms(blocks, slot_coords, live_mask, x_col, x_row)
    whole_row = lax.psum(row_terms, "col")
    is_owner = (col_idx == row_idx // seg_ratio).astype(jnp.float32)
    placed = whole_row * is_owner
    return lax.psum_scatter(col_terms + placed, "row", scatter_dimension=1, tiled=True)


def solution(mesh):
    return jax.shard_map(
        local,
        mesh=mesh,
        in_specs=(
            P(None, ("col", "row")),
            P("row", "col", None, None, None),
            P("row", "col", None),
            P("row", "col"),
        ),
        out_specs=P(None, ("col", "row")),
        check_vma=False,
    )
```

profile of v0, /device:TPU:32, one launch (start us, length us, event | category | flops | bytes accessed | tf_op | source)
XLA Modules:
  0.0 276.1 jit_solution(18044098846579297185)
XLA Ops:
  6.5 0.0 all-reduce.3.cloned.1.call-start
  7.2 0.7 compare_and_fusion.1
  7.9 25.0 %all_gather.3 = f32[16,2048]{1,0:T(8,128)S(1)} all-gather(f32[16,128]{1,0:T(8,128)} %param.6), channel_id=1, replica_groups=mesh['row'=16,'col'=16] {'row'}, dimensions={1}, use_global_device_ids=true | all-gather | bytes 139264 | tf_op jit(solution)/shard_map/all_gather | solution.py:51
  32.9 0.8 gather_fusion.1
  33.7 15.5 %fusion.7 = f32[16,128,128]{2,0,1:T(8,128)S(1)} fusion(f32[1,1,128,128,128]{4,3,2,1,0:T(8,128)} %param.7, f32[128,16,128]{2,1,0:T(8,128)S(1)} %gather_fusion.1, pred[128]{0:T(512)(128)(4,1)S(1)} %get-tuple-element.12), kind=kOutput, calls=%fused_computation.7 | convolution fusion | flops 402915328 | bytes 10485888 | tf_op jit(solution)/shard_map/vsk,smk->vsm/dot_general | solution.py:23
  49.1 0.9 fusion.12
  50.1 0.7 copy.21
  50.8 0.7 copy_bitcast_fusion.2
  51.4 0.0 all-reduce.3.cloned.1.call-update
  51.5 0.0 reduce-scatter.2.cloned.1.call-start
  51.5 134.0 %all-reduce.3.cloned.1.call-done = (f32[16,16,128]{2,0,1:T(8,128)}, f32[16,2048]{1,0:T(8,128)}) async-done(((f32[16,16,128]{2,0,1:T(8,128)}, f32[16,2048]{1,0:T(8,128)}), (f32[16,16,128]{2,0,1:T(8,128)}, f32[16,2048]{1,0:T(8,128)})) %all-reduce.3.cloned.1.call-update) | async-done | bytes 262160 | tf_op jit(solution)/shard_map/psum | solution.py:11
  185.5 0.0 copy-start
  185.6 1.6 gather_fusion
  187.1 9.6 %fusion.4 = f32[16,128,128]{2,0,1:T(8,128)S(1)} fusion(f32[1,1,128,128,128]{4,3,2,1,0:T(8,128)} %param.7, f32[128,16,128]{2,1,0:T(8,128)S(1)} %gather_fusion, pred[128]{0:T(512)(128)(4,1)S(1)} %get-tuple-element.8), kind=kOutput, calls=%fused_computation.6 | convolution fusion | flops 402915328 | bytes 10485888 | tf_op jit(solution)/shard_map/vsm,smk->vsk/dot_general | solution.py:24
  196.8 0.9 fusion.14
  197.7 0.0 copy-done
  197.7 0.7 bitcast_add_fusion
  198.4 0.0 reduce-scatter.2.cloned.1.call-update
  198.4 70.9 %reduce-scatter.2.cloned.1.call-done = f32[16,128]{1,0:T(8,128)} async-done(((f32[16,2048]{1,0:T(8,128)}), f32[16,128]{1,0:T(8,128)}) %reduce-scatter.2.cloned.1.call-update) | async-done | bytes 8208 | tf_op jit(solution)/shard_map/reduce_scatter | solution.py:58
  (5 shorter events, 0.0 us)
Async XLA Ops:
  6.5 179.0 %all-reduce.3.cloned.1.call-start = ((), (), s32[]{:S(2)}) async-start(), calls=%async_computation.2 | async-start | bytes 524288 | tf_op jit(solution)/shard_map/psum | solution.py:11
  51.5 217.9 %reduce-scatter.2.cloned.1.call-start = ((), (), s32[]{:S(2)}) async-start(), calls=%async_computation.1 | async-start | bytes 139264 | tf_op jit(solution)/shard_map/reduce_scatter | solution.py:58
  185.5 12.1 %copy-start = (f32[16,2048]{1,0:T(8,128)S(1)}, f32[16,2048]{1,0:T(8,128)}, u32[]{:S(2)}) copy-start(f32[16,2048]{1,0:T(8,128)} %get-tuple-element.7) | copy-start | bytes 393220
Sparse Core Ops, SparseCore 0:
  51.6 133.9 all-reduce.2
  198.5 70.7 reduce-scatter.1
where the time goes:
time: 276 us
  waiting for transfers between devices  205 us (74%)
  matrix products  26.9 us (10%)
  blocking collectives  25 us (9%)
  between operations  14.1 us (5%)
  local copies, waits for them, and re-layouts  3.07 us (1%)
    psum x1, waiting for transfers between devices, from_root(): return lax.psum(kept, axis)  134 us
    reduce_scatter x1, waiting for transfers between devices, local(): lax.psum_scatter(col_terms + placed, 'row', scatter_dimension=1, tiled=True)  70.9 us
    all_gather x1, blocking collectives, local(): x_col = lax.all_gather(vectors, 'row', axis=1, tiled=True)  25 us
    dot_general x1, matrix products, slot_terms(): normal = jnp.einsum('vsk,smk->vsm', picked_col, blocks, precision=HIGH)  15.5 us
    dot_general x1, matrix products, slot_terms(): transposed = jnp.einsum('vsm,smk->vsk', picked_row, blocks, precision=HIGH)  9.6 us
  transfers between devices with their start and end apart: 2, of which 2 were waited for; matrix products, arithmetic and copies ran while one was open for 0% of the time, Pallas kernels for 0%

commit v1 on v0

--- a/solution.py
+++ b/solution.py
@@ -48,7 +48,8 @@
     slot_count = counts.reshape(())
     row_idx = lax.axis_index("row")
     col_idx = lax.axis_index("col")
-    x_col = lax.all_gather(vectors, "row", axis=1, tiled=True)
+    outgoing = jnp.stack([vectors] * lax.axis_size("row"))
+    x_col = jnp.concatenate(lax.all_to_all(outgoing, "row", 0, 0), axis=1)
     x_row = from_root(x_col, "col", row_idx // seg_ratio)
     live_mask = (jnp.arange(max_slots, dtype=jnp.int32) < slot_count).astype(jnp.float32)
     row_terms, col_terms = slot_terms(blocks, slot_coords, live_mask, x_col, x_row)

time: 276 us -> 267 us (0.967)
  blocking collectives: 25 us -> 0 us
  starting transfers between devices: 0.04 us -> 7.12 us
  waiting for transfers between devices: 205 us -> 212 us
    all_gather x1 -> x0, blocking collectives: 25 us -> none  [local(): x_col = lax.all_gather(vectors, 'row', axis=1, tiled=True)]
    all_to_all x0 -> x1, starting transfers between devices: none -> 7.03 us  [local(): x_col = jnp.concatenate(lax.all_to_all(outgoing, 'row', 0, 0), axis=1)]
    all_to_all x0 -> x1, waiting for transfers between devices: none -> 6.76 us  [local(): x_col = jnp.concatenate(lax.all_to_all(outgoing, 'row', 0, 0), axis=1)]
  transfers between devices with their start and end apart: 2 -> 3, of which waited for: 2 -> 3; matrix products, arithmetic and copies ran while one was open for 0% -> 0% of each run, Pallas kernels for 0% -> 0%
where the time goes in v1:
time: 267 us; the launch traced here: 266 us
  waiting for transfers between devices  212 us (79%)
  matrix products  26.9 us (10%)
  between operations  14.2 us (5%)
  starting transfers between devices  7.12 us (3%)
  local copies, waits for them, and re-layouts  4.39 us (2%)
    psum x1, waiting for transfers between devices, from_root(): return lax.psum(kept, axis)  134 us
    reduce_scatter x1, waiting for transfers between devices, local(): lax.psum_scatter(col_terms + placed, 'row', scatter_dimension=1, tiled=True)  70.9 us
    dot_general x1, matrix products, slot_terms(): normal = jnp.einsum('vsk,smk->vsm', picked_col, blocks, precision=HIGH)  15.5 us
    dot_general x1, matrix products, slot_terms(): transposed = jnp.einsum('vsm,smk->vsk', picked_row, blocks, precision=HIGH)  9.6 us
    all_to_all x1, starting transfers between devices, local(): x_col = jnp.concatenate(lax.all_to_all(outgoing, 'row', 0, 0), axis=1)  7.03 us
    all_to_all x1, waiting for transfers between devices, local(): x_col = jnp.concatenate(lax.all_to_all(outgoing, 'row', 0, 0), axis=1)  6.76 us
  transfers between devices with their start and end apart: 3, of which 3 were waited for; matrix products, arithmetic and copies ran while one was open for 0% of the time, Pallas kernels for 0%

profile of v1, /device:TPU:32, one launch (start us, length us, event | category | flops | bytes accessed | tf_op | source)
XLA Modules:
  0.0 266.3 jit_solution(1790296000401507476)
XLA Ops:
  6.5 1.4 stack.2
  7.9 7.0 %all-to-all-start = ((f32[16,16,128]{2,1,0:T(8,128)}), f32[16,16,128]{2,1,0:T(8,128)S(1)}, u32[]{:S(2)}, u32[]{:S(2)}) async-start(f32[16,16,128]{2,1,0:T(8,128)} %stack.2), calls=%async_computation | async-start | bytes 262144 | tf_op jit(solution)/shard_map/all_to_all | solution.py:52
  14.9 0.0 all-reduce.3.cloned.1.call-start
  15.0 0.7 compare_and_fusion.1
  16.3 6.8 %all-to-all-done = f32[16,16,128]{2,1,0:T(8,128)S(1)} async-done(((f32[16,16,128]{2,1,0:T(8,128)}), f32[16,16,128]{2,1,0:T(8,128)S(1)}, u32[]{:S(2)}, u32[]{:S(2)}) %all-to-all-start) | async-done | bytes 131104 | tf_op jit(solution)/shard_map/all_to_all | solution.py:52
  23.1 0.8 gather_fusion.1
  23.9 15.5 %fusion = f32[128,16,128]{2,1,0:T(8,128)S(1)} fusion(f32[1,1,128,128,128]{4,3,2,1,0:T(8,128)} %param.7, f32[128,16,128]{2,1,0:T(8,128)S(1)} %gather_fusion.1, pred[128]{0:T(512)(128)(4,1)S(1)} %get-tuple-element.12), kind=kOutput, calls=%fused_computation.2 | convolution fusion | flops 402915328 | bytes 10485888 | tf_op jit(solution)/shard_map/vsk,smk->vsm/dot_general | solution.py:23
  39.3 0.9 fusion.4
  40.3 0.7 copy.19
  41.0 0.7 broadcast_select_fusion
  41.6 0.0 all-reduce.3.cloned.1.call-update
  41.6 0.0 reduce-scatter.2.cloned.1.call-start
  41.7 134.0 %all-reduce.3.cloned.1.call-done = (f32[16,16,128]{2,0,1:T(8,128)}, f32[16,2048]{1,0:T(8,128)}) async-done(((f32[16,16,128]{2,0,1:T(8,128)}, f32[16,2048]{1,0:T(8,128)}), (f32[16,16,128]{2,0,1:T(8,128)}, f32[16,2048]{1,0:T(8,128)})) %all-reduce.3.cloned.1.call-update) | async-done | bytes 262160 | tf_op jit(solution)/shard_map/psum | solution.py:11
  175.7 0.0 copy-start
  175.7 1.6 gather_fusion
  177.3 9.6 %fusion.2 = f32[128,16,128]{2,1,0:T(8,128)S(1)} fusion(f32[1,1,128,128,128]{4,3,2,1,0:T(8,128)} %param.7, f32[128,16,128]{2,1,0:T(8,128)S(1)} %gather_fusion, pred[128]{0:T(512)(128)(4,1)S(1)} %get-tuple-element.8), kind=kOutput, calls=%fused_computation.4 | convolution fusion | flops 402915328 | bytes 10485888 | tf_op jit(solution)/shard_map/vsm,smk->vsk/dot_general | solution.py:24
  186.9 0.9 fusion.7
  187.8 0.0 copy-done
  187.8 0.7 bitcast_add_fusion
  188.5 0.0 reduce-scatter.2.cloned.1.call-update
  188.5 70.9 %reduce-scatter.2.cloned.1.call-done = f32[16,128]{1,0:T(8,128)} async-done(((f32[16,2048]{1,0:T(8,128)}), f32[16,128]{1,0:T(8,128)}) %reduce-scatter.2.cloned.1.call-update) | async-done | bytes 8208 | tf_op jit(solution)/shard_map/reduce_scatter | solution.py:59
  (5 shorter events, 0.0 us)
Async XLA Ops:
  7.9 15.2 %all-to-all-start = ((f32[16,16,128]{2,1,0:T(8,128)}), f32[16,16,128]{2,1,0:T(8,128)S(1)}, u32[]{:S(2)}, u32[]{:S(2)}) async-start(f32[16,16,128]{2,1,0:T(8,128)} %stack.2), calls=%async_computation | async-start | bytes 262144 | tf_op jit(solution)/shard_map/all_to_all | solution.py:52
  14.9 160.7 %all-reduce.3.cloned.1.call-start = ((), (), s32[]{:S(2)}) async-start(), calls=%async_computation.3 | async-start | bytes 524288 | tf_op jit(solution)/shard_map/psum | solution.py:11
  41.6 217.8 %reduce-scatter.2.cloned.1.call-start = ((), (), s32[]{:S(2)}) async-start(), calls=%async_computation.2 | async-start | bytes 139264 | tf_op jit(solution)/shard_map/reduce_scatter | solution.py:59
  175.7 12.1 %copy-start = (f32[16,2048]{1,0:T(8,128)S(1)}, f32[16,2048]{1,0:T(8,128)}, u32[]{:S(2)}) copy-start(f32[16,2048]{1,0:T(8,128)} %get-tuple-element.7) | copy-start | bytes 393220
Sparse Core Ops, SparseCore 0:
  41.8 133.8 all-reduce.2
  188.7 70.7 reduce-scatter.1

commit v2 on v0

--- a/solution.py
+++ b/solution.py
@@ -2,13 +2,14 @@
 import jax.numpy as jnp
 from jax import lax
 from jax.sharding import PartitionSpec as P
+from jax.lax import all_gather
 
 HIGH = lax.Precision.HIGHEST
 
 
 def from_root(value, axis, source):
     kept = jnp.where(lax.axis_index(axis) == source, value, 0).astype(value.dtype)
-    return lax.psum(kept, axis)
+    return jnp.sum(all_gather(kept, axis), 0)
 
 
 def slot_terms(blocks, slot_coords, live_mask, x_col, x_row):

time: 276 us -> 320 us (1.16)
  waiting for transfers between devices: 205 us -> 247 us
    all_gather x0 -> x1, waiting for transfers between devices: none -> 49.6 us  [from_root(): return jnp.sum(all_gather(kept, axis), 0)]
    psum x1, waiting for transfers between devices: 134 us -> 125 us  [local(): whole_row = lax.psum(row_terms, 'col')]
  transfers between devices with their start and end apart: 2 -> 3, of which waited for: 2 -> 3; matrix products, arithmetic and copies ran while one was open for 0% -> 10% of each run, Pallas kernels for 0% -> 0%
where the time goes in v2:
time: 320 us
  waiting for transfers between devices  247 us (77%)
  matrix products  26.9 us (8%)
  blocking collectives  25 us (8%)
  between operations  13.9 us (4%)
  other arithmetic  4.65 us (1%)
    psum x1, waiting for transfers between devices, local(): whole_row = lax.psum(row_terms, 'col')  125 us
    reduce_scatter x1, waiting for transfers between devices, local(): lax.psum_scatter(col_terms + placed, 'row', scatter_dimension=1, tiled=True)  73.2 us
    all_gather x1, waiting for transfers between devices, from_root(): return jnp.sum(all_gather(kept, axis), 0)  49.6 us
    all_gather x1, blocking collectives, local(): x_col = lax.all_gather(vectors, 'row', axis=1, tiled=True)  25 us
    dot_general x1, matrix products, slot_terms(): normal = jnp.einsum('vsk,smk->vsm', picked_col, blocks, precision=HIGH)  15.5 us
    dot_general x1, matrix products, slot_terms(): transposed = jnp.einsum('vsm,smk->vsk', picked_row, blocks, precision=HIGH)  9.6 us
  transfers between devices with their start and end apart: 3, of which 3 were waited for; matrix products, arithmetic and copies ran while one was open for 10% of the time, Pallas kernels for 0%

profile of v2, /device:TPU:32, one launch (start us, length us, event | category | flops | bytes accessed | tf_op | source)
XLA Modules:
  0.0 320.1 jit_solution(3760047166257921980)
XLA Ops:
  6.5 0.0 all-gather.3.cloned.1.call-start
  6.5 25.0 %all_gather.9 = f32[16,2048]{1,0:T(8,128)S(1)} all-gather(f32[16,128]{1,0:T(8,128)} %param.6), channel_id=1, replica_groups=mesh['row'=16,'col'=16] {'row'}, dimensions={1}, use_global_device_ids=true | all-gather | bytes 139264 | tf_op jit(solution)/shard_map/all_gather | solution.py:52
  31.5 0.7 broadcast_select_fusion
  32.2 0.0 all-gather.3.cloned.1.call-update
  32.2 0.0 all-reduce.2.cloned.1.call-start
  32.9 0.7 compare_and_fusion
  33.6 0.8 gather_fusion.1
  34.4 15.5 %fusion.7 = f32[16,128,128]{2,0,1:T(8,128)S(1)} fusion(f32[1,1,128,128,128]{4,3,2,1,0:T(8,128)} %param.7, f32[128,16,128]{2,1,0:T(8,128)S(1)} %gather_fusion.1, pred[128]{0:T(512)(128)(4,1)S(1)} %get-tuple-element.6), kind=kOutput, calls=%fused_computation.7 | convolution fusion | flops 402915328 | bytes 10485888 | tf_op jit(solution)/shard_map/vsk,smk->vsm/dot_general | solution.py:24
  49.9 0.9 fusion.12
  50.8 0.7 copy.21
  51.5 0.0 all-reduce.2.cloned.1.call-update
  51.5 0.0 reduce-scatter.2.cloned.1.call-start
  51.6 49.6 %all-gather.3.cloned.1.call-done = f32[256,2048]{1,0:T(8,128)} async-done(((f32[16,2048]{1,0:T(8,128)}), f32[256,2048]{1,0:T(8,128)}) %all-gather.3.cloned.1.call-update) | async-done | bytes 2097168 | tf_op jit(solution)/shard_map/all_gather | solution.py:12
  101.2 1.7 reduce_sum.9
  102.9 0.8 gather_fusion
  103.7 9.6 %fusion.4 = f32[16,128,128]{2,0,1:T(8,128)S(1)} fusion(f32[1,1,128,128,128]{4,3,2,1,0:T(8,128)} %param.7, f32[128,16,128]{2,1,0:T(8,128)S(1)} %gather_fusion, pred[128]{0:T(512)(128)(4,1)S(1)} %get-tuple-element.10), kind=kOutput, calls=%fused_computation.6 | convolution fusion | flops 402915328 | bytes 10485888 | tf_op jit(solution)/shard_map/vsm,smk->vsk/dot_general | solution.py:25
  113.3 0.9 fusion.14
  114.2 124.6 %all-reduce.2.cloned.1.call-done = f32[16,2048]{1,0:T(8,128)} async-done(((f32[16,2048]{1,0:T(8,128)}), f32[16,2048]{1,0:T(8,128)}) %all-reduce.2.cloned.1.call-update) | async-done | bytes 131088 | tf_op jit(solution)/shard_map/psum | solution.py:56
  238.8 1.6 bitcast_add_fusion
  240.4 0.0 reduce-scatter.2.cloned.1.call-update
  240.4 73.2 %reduce-scatter.2.cloned.1.call-done = f32[16,128]{1,0:T(8,128)} async-done(((f32[16,2048]{1,0:T(8,128)}), f32[16,128]{1,0:T(8,128)}) %reduce-scatter.2.cloned.1.call-update) | async-done | bytes 8208 | tf_op jit(solution)/shard_map/reduce_scatter | solution.py:59
  (7 shorter events, 0.0 us)
Async XLA Ops:
  6.5 94.7 %all-gather.3.cloned.1.call-start = ((), (), s32[]{:S(2)}) async-start(), calls=%async_computation.3 | async-start | bytes 2228224 | tf_op jit(solution)/shard_map/all_gather | solution.py:12
  32.2 206.6 %all-reduce.2.cloned.1.call-start = ((), (), s32[]{:S(2)}) async-start(), calls=%async_computation.1 | async-start | bytes 262144 | tf_op jit(solution)/shard_map/psum | solution.py:56
  51.5 262.1 %reduce-scatter.2.cloned.1.call-start = ((), (), s32[]{:S(2)}) async-start(), calls=%async_computation.2 | async-start | bytes 139264 | tf_op jit(solution)/shard_map/reduce_scatter | solution.py:59
Sparse Core Ops, SparseCore 0:
  32.3 68.8 all-gather.2
  103.8 134.9 all-reduce.1
  242.7 70.8 reduce-scatter.1
